TPU v7x, 128 devices: a whole 4x4x4 slice. The times are simulated.
128 devices in a mesh: pair: 8 (over x, core), ints: 16 (over y, z).
Axes of the slice: x: 4, y: 4, z: 4, core: 2. Of those that a mesh axis runs over, the one named last changes fastest.
Arguments:
- t2: bfloat16 [4096, 8192], P('pair', 'ints'), may hold values from -6 to 6
- t2_live: int32 [8, 64], P('pair', 'ints'), may hold values 0 or 1
- int_tiles: int32 [5120, 2], P('ints'), may hold values from 0 to 63
- integrals: bfloat16 [5120, 128, 128], P('ints'), may hold values from -0.0625 to 0.0625
- cycle_w: bfloat16 [4096, 4096], P('pair'), may hold values from -0.09375 to 0.09375
- res_live: int32 [8, 64], P('pair', 'ints'), may hold values 0 or 1
Outputs:
- residual: float32 [4096, 8192], P('pair', 'ints')
All inputs are finite; a program needn't handle non-finite values. No bound on the sum of `t2_live` or of `res_live` on one device may be relied on, other than what follows from the above.
Results may differ from a plain program's by a relative error of at most 0.0003.
Values may be sent and summed in bfloat16 or wider, within the bound.
No kernel may reach another device: no remote copies, remote signals or barrier semaphores. Data moves between devices by JAX's collectives and lax.ppermute only.
A program may use at most 192 MiB of HBM per device.

v0:
```python
import jax
import jax.numpy as jnp
from jax import lax
from jax.sharding import PartitionSpec as P


def local(t2, t2_live, int_tiles, integrals, cycle_w, res_live):
    rows_here = t2.shape[0]
    tile_size = integrals.shape[1]
    tiles_here = t2.shape[1] // tile_size
    live_mask = t2_live[0].astype(t2.dtype)
    amps = (t2.reshape(rows_here, tiles_here, tile_size) * live_mask[None, :, None]).reshape(
        rows_here, tiles_here * tile_size
    )
    block_amps = lax.all_gather(amps, "ints", axis=1, tiled=True)
    tiles_all = block_amps.shape[1] // tile_size
    amps_tiled = block_amps.reshape(rows_here, tiles_all, tile_size)
    count_here = integrals.shape[0]
    group_size = 64
    tile_groups = int_tiles.reshape(count_here // group_size, group_size, 2)
    int_groups = integrals.reshape(count_here // group_size, group_size, tile_size, tile_size)
    tile_ids = jnp.arange(tiles_all, dtype=jnp.int32)

    def ladder_step(partial_value, entry):
        pairs_uv, blocks = entry
        source_table = (pairs_uv[:, 0:1] == tile_ids[None, :]).astype(jnp.bfloat16)
        target_table = (pairs_uv[:, 1:2] == tile_ids[None, :]).astype(jnp.float32)
        picked = jnp.einsum(
            "jt,ptc->jpc", source_table, amps_tiled, preferred_element_type=jnp.float32
        ).astype(jnp.bfloat16)
        product = jnp.einsum("jpc,jcd->jpd", picked, blocks, preferred_element_type=jnp.float32)
        partial_value = partial_value + jnp.einsum(
            "jv,jpd->vpd", target_table, product, precision=lax.Precision.HIGHEST
        )
        return (partial_value, None)

    start_sum = jnp.zeros((tiles_all, rows_here, tile_size), jnp.float32)
    partial_value, _ = lax.scan(ladder_step, start_sum, (tile_groups, int_groups))
    summed = lax.psum(partial_value, "ints")
    owned = lax.dynamic_slice_in_dim(summed, lax.axis_index("ints") * tiles_here, tiles_here, 0)
    ladder = owned.transpose(1, 0, 2).reshape(rows_here, tiles_here * tile_size)
    cycle_term = jnp.dot(
        cycle_w,
        lax.all_gather(amps, "pair", axis=0, tiled=True),
        preferred_element_type=jnp.float32,
    )
    keep_mask = jnp.repeat(res_live[0], tile_size).astype(jnp.float32)[None, :]
    return keep_mask * (ladder + cycle_term)


def solution(mesh):
    placed = (
        P("pair", "ints"),
        P("pair", "ints"),
        P("ints", None),
        P("ints", None, None),
        P("pair", None),
        P("pair", "ints"),
    )
    return jax.shard_map(
        local, mesh=mesh, in_specs=placed, out_specs=P("pair", "ints"), check_vma=False
    )
```

profile of v0, /device:TPU:1, one launch (start us, length us, event | category | flops | bytes accessed | tf_op | source)
XLA Modules:
  0.0 551.5 jit_solution(12331240370962497261)
XLA Ops:
  7.4 0.0 all-gather.3.cloned.1.call-start
  7.4 0.7 convert_bitcast_fusion
  8.0 0.1 broadcast_bitcast_fusion.1
  8.1 1.9 broadcast_multiply_fusion
  10.0 0.0 all-gather.3.cloned.1.call-update
  10.0 0.0 all-reduce.2.cloned.1.call-start
  10.1 0.8 reshape.30
  10.8 80.4 %all-gather.3.cloned.1.call-done = bf16[512,8192]{1,0:T(8,128)(2,1)} async-done(((bf16[512,512]{1,0:T(8,128)(2,1)}), bf16[512,8192]{1,0:T(8,128)(2,1)}) %all-gather.3.cloned.1.call-update) | async-done | bytes 8388624 | tf_op jit(solution)/shard_map/all_gather | solution.py:15
  91.2 9.3 %copy.15 = bf16[64,8,64,128]{3,2,1,0:T(8,128)(2,1)} copy(bf16[64,8,64,128]{3,1,2,0:T(8,128)(2,1)} %bitcast.55) | data formatting | bytes 16777216
  100.5 213.6 %while.12 = (s32[]{:T(128)}, f32[64,512,128]{2,0,1:T(8,128)}, s32[5,64,2]{1,0,2:T(8,128)S(1)}, bf16[512,64,128]{2,1,0:T(8,128)(2,1)}, bf16[5,64,128,128]{3,2,1,0:T(8,128)(2,1)}, /*index=5*/s32[]{:T(128)}, s32[]{:T(128)}) while((s32[]{:T(128)}, f32[64,512,128]{2,0,1:T(8,128)}, s32[5,64,2]{1,0,2:T(8,128)S(1)}, ...), condition=%wide.region_1.2_spmd.clone.clone, body=%wide.region_0.1_spmd.clone.clone.sunk | while | flops 4840235008 | bytes 94374496 | solution.py:38
  100.5 5.8 %fusion.34 = bf16[64,512,128]{2,0,1:T(8,128)(2,1)S(1)} fusion(bf16[512,64,128]{2,1,0:T(8,128)(2,1)} %get-tuple-element.146, s32[64]{0:T(128)S(1)} %get-tuple-element.127), kind=kOutput, calls=%fused_computation.12.clone.1 | convolution fusion | flops 536875008 | bytes 16777472 | tf_op jit(solution)/shard_map/while/body/eval_jaxpr/jt,ptc->jpc/dot_general | solution.py:28
  106.3 13.9 %fusion.35 = f32[64,512,128]{2,1,0:T(8,128)} fusion(bf16[64,512,128]{2,0,1:T(8,128)(2,1)S(1)} %fusion.34, bf16[5,64,128,128]{3,2,1,0:T(8,128)(2,1)} %get-tuple-element.147, s32[]{:T(128)S(6)} %copy.28), kind=kOutput, calls=%fused_computation.5.clone.1 | convolution fusion | flops 1073741824 | bytes 27262980 | tf_op jit(solution)/shard_map/while/body/eval_jaxpr/jpc,jcd->jpd/dot_general | solution.py:31
  120.2 20.4 %select_add_fusion.2 = f32[64,512,128]{2,0,1:T(8,128)} fusion(f32[64,512,128]{2,0,1:T(8,128)} %get-tuple-element.137, f32[64,512,128]{2,1,0:T(8,128)} %fusion.35, pred[]{:T(512)S(6)} %compare.3, s32[64]{0:T(128)S(1)} %get-tuple-element.128), kind=kOutput, calls=%fused_computation.4.clone.1 | convolution fusion | flops 3229618176 | bytes 50331904 | tf_op jit(solution)/shard_map/while/body/eval_jaxpr/jv,jpd->vpd/dot_general | solution.py:32
  140.6 5.8 %fusion.34 = bf16[64,512,128]{2,0,1:T(8,128)(2,1)S(1)} fusion(bf16[512,64,128]{2,1,0:T(8,128)(2,1)} %get-tuple-element.146, s32[64]{0:T(128)S(1)} %get-tuple-element.127), kind=kOutput, calls=%fused_computation.12.clone.1 | convolution fusion | flops 536875008 | bytes 16777472 | tf_op jit(solution)/shard_map/while/body/eval_jaxpr/jt,ptc->jpc/dot_general | solution.py:28
  146.4 13.9 %fusion.35 = f32[64,512,128]{2,1,0:T(8,128)} fusion(bf16[64,512,128]{2,0,1:T(8,128)(2,1)S(1)} %fusion.34, bf16[5,64,128,128]{3,2,1,0:T(8,128)(2,1)} %get-tuple-element.147, s32[]{:T(128)S(6)} %copy.28), kind=kOutput, calls=%fused_computation.5.clone.1 | convolution fusion | flops 1073741824 | bytes 27262980 | tf_op jit(solution)/shard_map/while/body/eval_jaxpr/jpc,jcd->jpd/dot_general | solution.py:31
  160.3 23.7 %select_add_fusion.2 = f32[64,512,128]{2,0,1:T(8,128)} fusion(f32[64,512,128]{2,0,1:T(8,128)} %get-tuple-element.137, f32[64,512,128]{2,1,0:T(8,128)} %fusion.35, pred[]{:T(512)S(6)} %compare.3, s32[64]{0:T(128)S(1)} %get-tuple-element.128), kind=kOutput, calls=%fused_computation.4.clone.1 | convolution fusion | flops 3229618176 | bytes 50331904 | tf_op jit(solution)/shard_map/while/body/eval_jaxpr/jv,jpd->vpd/dot_general | solution.py:32
  184.0 5.8 %fusion.34 = bf16[64,512,128]{2,0,1:T(8,128)(2,1)S(1)} fusion(bf16[512,64,128]{2,1,0:T(8,128)(2,1)} %get-tuple-element.146, s32[64]{0:T(128)S(1)} %get-tuple-element.127), kind=kOutput, calls=%fused_computation.12.clone.1 | convolution fusion | flops 536875008 | bytes 16777472 | tf_op jit(solution)/shard_map/while/body/eval_jaxpr/jt,ptc->jpc/dot_general | solution.py:28
  189.8 13.9 %fusion.35 = f32[64,512,128]{2,1,0:T(8,128)} fusion(bf16[64,512,128]{2,0,1:T(8,128)(2,1)S(1)} %fusion.34, bf16[5,64,128,128]{3,2,1,0:T(8,128)(2,1)} %get-tuple-element.147, s32[]{:T(128)S(6)} %copy.28), kind=kOutput, calls=%fused_computation.5.clone.1 | convolution fusion | flops 1073741824 | bytes 27262980 | tf_op jit(solution)/shard_map/while/body/eval_jaxpr/jpc,jcd->jpd/dot_general | solution.py:31
  203.7 23.7 %select_add_fusion.2 = f32[64,512,128]{2,0,1:T(8,128)} fusion(f32[64,512,128]{2,0,1:T(8,128)} %get-tuple-element.137, f32[64,512,128]{2,1,0:T(8,128)} %fusion.35, pred[]{:T(512)S(6)} %compare.3, s32[64]{0:T(128)S(1)} %get-tuple-element.128), kind=kOutput, calls=%fused_computation.4.clone.1 | convolution fusion | flops 3229618176 | bytes 50331904 | tf_op jit(solution)/shard_map/while/body/eval_jaxpr/jv,jpd->vpd/dot_general | solution.py:32
  227.4 5.8 %fusion.34 = bf16[64,512,128]{2,0,1:T(8,128)(2,1)S(1)} fusion(bf16[512,64,128]{2,1,0:T(8,128)(2,1)} %get-tuple-element.146, s32[64]{0:T(128)S(1)} %get-tuple-element.127), kind=kOutput, calls=%fused_computation.12.clone.1 | convolution fusion | flops 536875008 | bytes 16777472 | tf_op jit(solution)/shard_map/while/body/eval_jaxpr/jt,ptc->jpc/dot_general | solution.py:28
  233.1 13.9 %fusion.35 = f32[64,512,128]{2,1,0:T(8,128)} fusion(bf16[64,512,128]{2,0,1:T(8,128)(2,1)S(1)} %fusion.34, bf16[5,64,128,128]{3,2,1,0:T(8,128)(2,1)} %get-tuple-element.147, s32[]{:T(128)S(6)} %copy.28), kind=kOutput, calls=%fused_computation.5.clone.1 | convolution fusion | flops 1073741824 | bytes 27262980 | tf_op jit(solution)/shard_map/while/body/eval_jaxpr/jpc,jcd->jpd/dot_general | solution.py:31
  247.1 23.7 %select_add_fusion.2 = f32[64,512,128]{2,0,1:T(8,128)} fusion(f32[64,512,128]{2,0,1:T(8,128)} %get-tuple-element.137, f32[64,512,128]{2,1,0:T(8,128)} %fusion.35, pred[]{:T(512)S(6)} %compare.3, s32[64]{0:T(128)S(1)} %get-tuple-element.128), kind=kOutput, calls=%fused_computation.4.clone.1 | convolution fusion | flops 3229618176 | bytes 50331904 | tf_op jit(solution)/shard_map/while/body/eval_jaxpr/jv,jpd->vpd/dot_general | solution.py:32
  270.7 5.8 %fusion.34 = bf16[64,512,128]{2,0,1:T(8,128)(2,1)S(1)} fusion(bf16[512,64,128]{2,1,0:T(8,128)(2,1)} %get-tuple-element.146, s32[64]{0:T(128)S(1)} %get-tuple-element.127), kind=kOutput, calls=%fused_computation.12.clone.1 | convolution fusion | flops 536875008 | bytes 16777472 | tf_op jit(solution)/shard_map/while/body/eval_jaxpr/jt,ptc->jpc/dot_general | solution.py:28
  276.5 13.9 %fusion.35 = f32[64,512,128]{2,1,0:T(8,128)} fusion(bf16[64,512,128]{2,0,1:T(8,128)(2,1)S(1)} %fusion.34, bf16[5,64,128,128]{3,2,1,0:T(8,128)(2,1)} %get-tuple-element.147, s32[]{:T(128)S(6)} %copy.28), kind=kOutput, calls=%fused_computation.5.clone.1 | convolution fusion | flops 1073741824 | bytes 27262980 | tf_op jit(solution)/shard_map/while/body/eval_jaxpr/jpc,jcd->jpd/dot_general | solution.py:31
  290.4 23.7 %select_add_fusion.2 = f32[64,512,128]{2,0,1:T(8,128)} fusion(f32[64,512,128]{2,0,1:T(8,128)} %get-tuple-element.137, f32[64,512,128]{2,1,0:T(8,128)} %fusion.35, pred[]{:T(512)S(6)} %compare.3, s32[64]{0:T(128)S(1)} %get-tuple-element.128), kind=kOutput, calls=%fused_computation.4.clone.1 | convolution fusion | flops 3229618176 | bytes 50331904 | tf_op jit(solution)/shard_map/while/body/eval_jaxpr/jv,jpd->vpd/dot_general | solution.py:32
  314.1 0.0 copy-start
  314.1 0.0 all-reduce.2.cloned.1.call-update
  314.1 0.2 all-gather.5.cloned.1.call-start
  314.4 0.3 all-gather.5.cloned.1.call-update
  314.7 0.0 copy-done
  314.8 0.1 broadcast_bitcast_fusion
  314.8 219.9 %all-reduce.2.cloned.1.call-done = f32[64,512,128]{2,0,1:T(8,128)} async-done(((f32[64,512,128]{2,0,1:T(8,128)}), f32[64,512,128]{2,0,1:T(8,128)}) %all-reduce.2.cloned.1.call-update) | async-done | bytes 16777232 | tf_op jit(solution)/shard_map/psum | solution.py:39
  534.7 1.8 dynamic-slice_bitcast_fusion
  536.5 0.4 copy.10
  536.9 0.0 all-gather.5.cloned.1.call-done
  536.9 5.8 %fusion.18 = f32[512,512]{0,1:T(8,128)S(1)} fusion(f32[512,512]{0,1:T(8,128)S(1)} %bitcast.56, bf16[4096,512]{1,0:T(8,128)(2,1)} %all-gather.5.cloned.1.call-done, bf16[512,4096]{1,0:T(8,128)(2,1)} %param.12, f32[512]{0:T(512)S(1)} %broadcast_bitcast_fusion), kind=kOutput, calls=%fused_computation.21 | convolution fusion | flops 2148007936 | bytes 10487808 | tf_op jit(solution)/shard_map/dot_general | solution.py:42
  542.8 1.3 copy.11
  (12 shorter events, 0.1 us)
Async XLA Ops:
  7.4 83.8 %all-gather.3.cloned.1.call-start = ((), (), s32[]{:S(2)}) async-start(), calls=%async_computation | async-start | bytes 8912896 | tf_op jit(solution)/shard_map/all_gather | solution.py:15
  10.0 524.7 %all-reduce.2.cloned.1.call-start = ((), (), s32[]{:S(2)}) async-start(), calls=%async_computation.1 | async-start | bytes 33554432 | tf_op jit(solution)/shard_map/psum | solution.py:39
  314.1 0.7 copy-start
  314.1 222.8 %all-gather.5.cloned.1.call-start = ((), (), s32[]{:S(2)}) async-start(), calls=%async_computation.2 | async-start | bytes 4718592 | tf_op jit(solution)/shard_map/all_gather | solution.py:44
Sparse Core Ops, SparseCore 0:
  10.3 80.8 all-gather.2
  314.2 220.4 all-reduce.1
Sparse Core Ops, SparseCore 1:
  316.3 32.4 all-gather.4
where the time goes:
time: 552 us
  waiting for transfers between devices  301 us (55%)
  matrix products  219 us (40%)
  between operations  14.9 us (3%)
  local copies, waits for them, and re-layouts  13.7 us (2%)
    psum x1, waiting for transfers between devices, local(): summed = lax.psum(partial_value, 'ints')  220 us
    dot_general x5, matrix products, ladder_step(): jnp.einsum('jv,jpd->vpd', target_table, product, precision=lax.Precision....  115 us
    all_gather x1, waiting for transfers between devices, local(): block_amps = lax.all_gather(amps, 'ints', axis=1, tiled=True)  80.4 us
    dot_general x5, matrix products, ladder_step(): jnp.einsum('jpc,jcd->jpd', picked, blocks, preferred_element_type=jnp.flo...  69.7 us
    dot_general x5, matrix products, ladder_step(): jnp.einsum('jt,ptc->jpc', source_table, amps_tiled, preferred_element_typ...  28.8 us
  transfers between devices with their start and end apart: 3, of which 2 were waited for; matrix products, arithmetic and copies ran while one was open for 1% of the time, Pallas kernels for 0%

commit v1 on v0

--- a/solution.py
+++ b/solution.py
@@ -12,7 +12,21 @@
     amps = (t2.reshape(rows_here, tiles_here, tile_size) * live_mask[None, :, None]).reshape(
         rows_here, tiles_here * tile_size
     )
-    block_amps = lax.all_gather(amps, "ints", axis=1, tiled=True)
+    ways, here, step = (lax.axis_size("ints"), lax.axis_index("ints"), amps.shape[1])
+    dims = [n * ways if d == 1 else n for d, n in enumerate(amps.shape)]
+    full = lax.dynamic_update_slice_in_dim(jnp.zeros(dims, amps.dtype), amps, here * step, axis=1)
+    going_up = going_down = amps
+    for far in range(1, ways // 2 + 1):
+        going_up = lax.ppermute(going_up, "ints", [(d, (d + 1) % ways) for d in range(ways)])
+        full = lax.dynamic_update_slice_in_dim(full, going_up, (here - far) % ways * step, axis=1)
+        if 2 * far < ways:
+            going_down = lax.ppermute(
+                going_down, "ints", [(d, (d - 1) % ways) for d in range(ways)]
+            )
+            full = lax.dynamic_update_slice_in_dim(
+                full, going_down, (here + far) % ways * step, axis=1
+            )
+    block_amps = full
     tiles_all = block_amps.shape[1] // tile_size
     amps_tiled = block_amps.reshape(rows_here, tiles_all, tile_size)
     count_here = integrals.shape[0]

time: 552 us -> 590 us (1.069)
  starting transfers between devices: 0.27 us -> 35.3 us
  local copies, waits for them, and re-layouts: 13.7 us -> 38.9 us
  waiting for transfers between devices: 301 us -> 279 us
    all_gather x1 -> x0, waiting for transfers between devices: 80.4 us -> none  [local(): block_amps = lax.all_gather(amps, 'ints', axis=1, tiled=True)]
    ppermute x0 -> x15, waiting for transfers between devices: none -> 55.3 us  [the longest x8 55.3 us: local(): lax.ppermute(going_up, 'ints', [(d, (d + 1) % ways) for d in range(ways)])]
    ppermute x0 -> x15, starting transfers between devices: none -> 35 us  [the longest x7 32.5 us: local(): lax.ppermute(going_down, 'ints', [(d, (d - 1) % ways) for d in range(ways)])]
    dynamic_update_slice x0 -> x15, local copies, waits for them, and re-layouts: none -> 20.7 us  [the longest x8 11.2 us: local(): lax.dynamic_update_slice_in_dim(full, going_up, (here - far) % ways * ste...]
  transfers between devices with their start and end apart: 3 -> 17, of which waited for: 2 -> 8; matrix products, arithmetic and copies ran while one was open for 1% -> 4% of each run, Pallas kernels for 0% -> 0%
where the time goes in v1:
time: 590 us; the launch traced here: 589 us
  waiting for transfers between devices  279 us (47%)
  matrix products  219 us (37%)
  local copies, waits for them, and re-layouts  38.9 us (7%)
  starting transfers between devices  35.3 us (6%)
  between operations  15 us (3%)
    psum x1, waiting for transfers between devices, local(): summed = lax.psum(partial_value, 'ints')  223 us
    dot_general x5, matrix products, ladder_step(): jnp.einsum('jv,jpd->vpd', target_table, product, precision=lax.Precision....  115 us
    dot_general x5, matrix products, ladder_step(): jnp.einsum('jpc,jcd->jpd', picked, blocks, preferred_element_type=jnp.flo...  69.6 us
    ppermute x8, waiting for transfers between devices, local(): lax.ppermute(going_up, 'ints', [(d, (d + 1) % ways) for d in range(ways)])  55.3 us
    ppermute x7, starting transfers between devices, local(): lax.ppermute(going_down, 'ints', [(d, (d - 1) % ways) for d in range(ways)])  32.5 us
    dot_general x5, matrix products, ladder_step(): jnp.einsum('jt,ptc->jpc', source_table, amps_tiled, preferred_element_typ...  28.8 us
  transfers between devices with their start and end apart: 17, of which 8 were waited for; matrix products, arithmetic and copies ran while one was open for 4% of the time, Pallas kernels for 0%

profile of v1, /device:TPU:1, one launch (start us, length us, event | category | flops | bytes accessed | tf_op | source)
XLA Modules:
  0.0 588.7 jit_solution(15880532895111023995)
XLA Ops:
  7.4 0.7 convert_bitcast_fusion
  8.1 0.1 broadcast_bitcast_fusion.1
  8.2 4.3 broadcast_in_dim.15
  12.5 0.9 constant_dynamic-update-slice_fusion.15
  13.4 2.5 collective-permute-start
  15.9 4.5 collective-permute-start.1
  20.4 11.6 %collective-permute-done = bf16[512,512]{1,0:T(8,128)(2,1)S(1)} collective-permute-done((bf16[512,512]{1,0:T(8,128)(2,1)S(1)}, bf16[512,512]{1,0:T(8,128)(2,1)S(1)}, u32[]{:S(2)}, u32[]{:S(2)}) %collective-permute-start) | collective-permute-done | bytes 524320 | tf_op jit(solution)/shard_map/ppermute | solution.py:20
  32.1 4.8 collective-permute-start.3
  36.9 10.7 %collective-permute-done.2 = bf16[512,512]{1,0:T(8,128)(2,1)S(1)} collective-permute-done((bf16[512,512]{1,0:T(8,128)(2,1)S(1)}, bf16[512,512]{1,0:T(8,128)(2,1)S(1)}, u32[]{:S(2)}, u32[]{:S(2)}) %collective-permute-start.2) | collective-permute-done | bytes 524320 | tf_op jit(solution)/shard_map/ppermute | solution.py:20
  47.6 4.8 collective-permute-start.5
  52.4 9.7 %collective-permute-done.4 = bf16[512,512]{1,0:T(8,128)(2,1)S(1)} collective-permute-done((bf16[512,512]{1,0:T(8,128)(2,1)S(1)}, bf16[512,512]{1,0:T(8,128)(2,1)S(1)}, u32[]{:S(2)}, u32[]{:S(2)}) %collective-permute-start.4) | collective-permute-done | bytes 524320 | tf_op jit(solution)/shard_map/ppermute | solution.py:20
  62.2 4.8 collective-permute-start.7
  67.0 8.9 %collective-permute-done.6 = bf16[512,512]{1,0:T(8,128)(2,1)S(1)} collective-permute-done((bf16[512,512]{1,0:T(8,128)(2,1)S(1)}, bf16[512,512]{1,0:T(8,128)(2,1)S(1)}, u32[]{:S(2)}, u32[]{:S(2)}) %collective-permute-start.6) | collective-permute-done | bytes 524320 | tf_op jit(solution)/shard_map/ppermute | solution.py:20
  75.9 0.8 copy-done.4
  76.7 4.0 collective-permute-start.9
  80.7 8.0 %collective-permute-done.8 = bf16[512,512]{1,0:T(8,128)(2,1)} collective-permute-done((bf16[512,512]{1,0:T(8,128)(2,1)S(1)}, bf16[512,512]{1,0:T(8,128)(2,1)}, u32[]{:S(2)}, u32[]{:S(2)}) %collective-permute-start.8) | collective-permute-done | bytes 524320 | tf_op jit(solution)/shard_map/ppermute | solution.py:20
  88.7 0.1 reshape.30
  88.8 0.9 constant_dynamic-update-slice_fusion.14
  89.6 1.9 constant_dynamic-update-slice_fusion.13
  91.6 1.9 constant_dynamic-update-slice_fusion.12
  93.5 4.7 collective-permute-start.11
  98.3 2.0 constant_dynamic-update-slice_fusion.11
  100.2 0.6 collective-permute-done.10
  100.8 0.8 constant_dynamic-update-slice_fusion.10
  101.7 0.9 constant_dynamic-update-slice_fusion.9
  102.6 1.9 constant_dynamic-update-slice_fusion.8
  104.5 2.0 constant_dynamic-update-slice_fusion.7
  106.4 4.8 collective-permute-start.13
  111.2 1.9 constant_dynamic-update-slice_fusion.6
  113.2 0.9 constant_dynamic-update-slice_fusion.5
  114.1 1.9 constant_dynamic-update-slice_fusion.4
  116.0 0.9 constant_dynamic-update-slice_fusion.3
  116.9 0.9 constant_dynamic-update-slice_fusion.2
  117.8 0.9 constant_dynamic-update-slice_fusion.1
  118.8 5.8 collective-permute-done.14
  124.5 0.9 constant_dynamic-update-slice_fusion
  125.4 9.3 %copy.15 = bf16[64,8,64,128]{3,2,1,0:T(8,128)(2,1)} copy(bf16[64,8,64,128]{3,1,2,0:T(8,128)(2,1)} %bitcast.17) | data formatting | bytes 16777216
  134.8 213.5 %while.12 = (s32[]{:T(128)}, f32[64,512,128]{2,0,1:T(8,128)}, s32[5,64,2]{1,0,2:T(8,128)S(1)}, bf16[512,64,128]{2,1,0:T(8,128)(2,1)}, bf16[5,64,128,128]{3,2,1,0:T(8,128)(2,1)}, /*index=5*/s32[]{:T(128)}, s32[]{:T(128)}) while((s32[]{:T(128)}, f32[64,512,128]{2,0,1:T(8,128)}, s32[5,64,2]{1,0,2:T(8,128)S(1)}, ...), condition=%wide.region_1.2_spmd.clone.clone, body=%wide.region_0.1_spmd.clone.clone.sunk | while | flops 4840235008 | bytes 94375000 | solution.py:52
  134.8 5.8 fusion.34
  140.5 13.9 %fusion.35 = f32[64,512,128]{2,1,0:T(8,128)} fusion(bf16[64,512,128]{2,0,1:T(8,128)(2,1)S(1)} %fusion.34, bf16[5,64,128,128]{3,2,1,0:T(8,128)(2,1)} %get-tuple-element.149, s32[]{:T(128)} %get-tuple-element.138), kind=kOutput, calls=%fused_computation.5.clone.1 | convolution fusion | flops 1073741824 | bytes 27263488 | tf_op jit(solution)/shard_map/while/body/eval_jaxpr/jpc,jcd->jpd/dot_general | solution.py:45
  154.5 20.4 %select_add_fusion.2 = f32[64,512,128]{2,0,1:T(8,128)} fusion(f32[64,512,128]{2,0,1:T(8,128)} %get-tuple-element.139, f32[64,512,128]{2,1,0:T(8,128)} %fusion.35, pred[]{:T(512)S(6)} %compare.18, s32[64]{0:T(128)S(1)} %get-tuple-element.130), kind=kOutput, calls=%fused_computation.4.clone.1 | convolution fusion | flops 3229618176 | bytes 50331904 | tf_op jit(solution)/shard_map/while/body/eval_jaxpr/jv,jpd->vpd/dot_general | solution.py:46
  174.9 5.8 fusion.34
  180.7 13.9 %fusion.35 = f32[64,512,128]{2,1,0:T(8,128)} fusion(bf16[64,512,128]{2,0,1:T(8,128)(2,1)S(1)} %fusion.34, bf16[5,64,128,128]{3,2,1,0:T(8,128)(2,1)} %get-tuple-element.149, s32[]{:T(128)} %get-tuple-element.138), kind=kOutput, calls=%fused_computation.5.clone.1 | convolution fusion | flops 1073741824 | bytes 27263488 | tf_op jit(solution)/shard_map/while/body/eval_jaxpr/jpc,jcd->jpd/dot_general | solution.py:45
  194.6 23.6 %select_add_fusion.2 = f32[64,512,128]{2,0,1:T(8,128)} fusion(f32[64,512,128]{2,0,1:T(8,128)} %get-tuple-element.139, f32[64,512,128]{2,1,0:T(8,128)} %fusion.35, pred[]{:T(512)S(6)} %compare.18, s32[64]{0:T(128)S(1)} %get-tuple-element.130), kind=kOutput, calls=%fused_computation.4.clone.1 | convolution fusion | flops 3229618176 | bytes 50331904 | tf_op jit(solution)/shard_map/while/body/eval_jaxpr/jv,jpd->vpd/dot_general | solution.py:46
  218.2 5.8 fusion.34
  224.0 13.9 %fusion.35 = f32[64,512,128]{2,1,0:T(8,128)} fusion(bf16[64,512,128]{2,0,1:T(8,128)(2,1)S(1)} %fusion.34, bf16[5,64,128,128]{3,2,1,0:T(8,128)(2,1)} %get-tuple-element.149, s32[]{:T(128)} %get-tuple-element.138), kind=kOutput, calls=%fused_computation.5.clone.1 | convolution fusion | flops 1073741824 | bytes 27263488 | tf_op jit(solution)/shard_map/while/body/eval_jaxpr/jpc,jcd->jpd/dot_general | solution.py:45
  237.9 23.6 %select_add_fusion.2 = f32[64,512,128]{2,0,1:T(8,128)} fusion(f32[64,512,128]{2,0,1:T(8,128)} %get-tuple-element.139, f32[64,512,128]{2,1,0:T(8,128)} %fusion.35, pred[]{:T(512)S(6)} %compare.18, s32[64]{0:T(128)S(1)} %get-tuple-element.130), kind=kOutput, calls=%fused_computation.4.clone.1 | convolution fusion | flops 3229618176 | bytes 50331904 | tf_op jit(solution)/shard_map/while/body/eval_jaxpr/jv,jpd->vpd/dot_general | solution.py:46
  261.6 5.8 fusion.34
  267.4 13.9 %fusion.35 = f32[64,512,128]{2,1,0:T(8,128)} fusion(bf16[64,512,128]{2,0,1:T(8,128)(2,1)S(1)} %fusion.34, bf16[5,64,128,128]{3,2,1,0:T(8,128)(2,1)} %get-tuple-element.149, s32[]{:T(128)} %get-tuple-element.138), kind=kOutput, calls=%fused_computation.5.clone.1 | convolution fusion | flops 1073741824 | bytes 27263488 | tf_op jit(solution)/shard_map/while/body/eval_jaxpr/jpc,jcd->jpd/dot_general | solution.py:45
  281.3 23.6 %select_add_fusion.2 = f32[64,512,128]{2,0,1:T(8,128)} fusion(f32[64,512,128]{2,0,1:T(8,128)} %get-tuple-element.139, f32[64,512,128]{2,1,0:T(8,128)} %fusion.35, pred[]{:T(512)S(6)} %compare.18, s32[64]{0:T(128)S(1)} %get-tuple-element.130), kind=kOutput, calls=%fused_computation.4.clone.1 | convolution fusion | flops 3229618176 | bytes 50331904 | tf_op jit(solution)/shard_map/while/body/eval_jaxpr/jv,jpd->vpd/dot_general | solution.py:46
  304.9 5.8 fusion.34
  310.7 13.9 %fusion.35 = f32[64,512,128]{2,1,0:T(8,128)} fusion(bf16[64,512,128]{2,0,1:T(8,128)(2,1)S(1)} %fusion.34, bf16[5,64,128,128]{3,2,1,0:T(8,128)(2,1)} %get-tuple-element.149, s32[]{:T(128)} %get-tuple-element.138), kind=kOutput, calls=%fused_computation.5.clone.1 | convolution fusion | flops 1073741824 | bytes 27263488 | tf_op jit(solution)/shard_map/while/body/eval_jaxpr/jpc,jcd->jpd/dot_general | solution.py:45
  324.6 23.6 %select_add_fusion.2 = f32[64,512,128]{2,0,1:T(8,128)} fusion(f32[64,512,128]{2,0,1:T(8,128)} %get-tuple-element.139, f32[64,512,128]{2,1,0:T(8,128)} %fusion.35, pred[]{:T(512)S(6)} %compare.18, s32[64]{0:T(128)S(1)} %get-tuple-element.130), kind=kOutput, calls=%fused_computation.4.clone.1 | convolution fusion | flops 3229618176 | bytes 50331904 | tf_op jit(solution)/shard_map/while/body/eval_jaxpr/jv,jpd->vpd/dot_general | solution.py:46
  348.3 0.0 all-reduce.2.cloned.1.call-update
  348.3 0.3 all-gather.2.cloned.1.call-start
  348.6 0.3 all-gather.2.cloned.1.call-update
  348.9 0.0 copy-done.7
  348.9 0.1 broadcast_bitcast_fusion
  349.0 223.0 %all-reduce.2.cloned.1.call-done = f32[64,512,128]{2,0,1:T(8,128)} async-done(((f32[64,512,128]{2,0,1:T(8,128)}), f32[64,512,128]{2,0,1:T(8,128)}) %all-reduce.2.cloned.1.call-update) | async-done | bytes 16777232 | tf_op jit(solution)/shard_map/psum | solution.py:53
  571.9 1.8 dynamic-slice_bitcast_fusion
  573.7 0.4 copy.10
  574.1 0.0 all-gather.2.cloned.1.call-done
  574.1 5.8 fusion.18
  580.0 1.3 copy.11
  (42 shorter events, 0.1 us)
Async XLA Ops:
  7.4 5.1 copy-start.1
  7.4 81.3 %copy-start.6 = (s32[320,2]{0,1:T(2,128)S(1)}, s32[320,2]{0,1:T(2,128)}, u32[]{:S(2)}) copy-start(s32[320,2]{0,1:T(2,128)} %param.10) | copy-start | bytes 7684
  7.4 564.6 %all-reduce.2.cloned.1.call-start = ((), (), s32[]{:S(2)}) async-start(), calls=%async_computation | async-start | bytes 33554432 | tf_op jit(solution)/shard_map/psum | solution.py:53
  13.4 121.4 %copy-start = (bf16[512,512]{1,0:T(8,128)(2,1)}, bf16[512,512]{1,0:T(8,128)(2,1)S(1)}, u32[]{:S(2)}) copy-start(bf16[512,512]{1,0:T(8,128)(2,1)S(1)} %get-tuple-element.93) | copy-start | bytes 1572868
  13.4 18.7 %collective-permute-start = (bf16[512,512]{1,0:T(8,128)(2,1)S(1)}, bf16[512,512]{1,0:T(8,128)(2,1)S(1)}, u32[]{:S(2)}, u32[]{:S(2)}) collective-permute-start(bf16[512,512]{1,0:T(8,128)(2,1)S(1)} %get-tuple-element.93), channel_id=1, source_target_pairs={{0,1},{1,2},{2,3},{3,4},{4,5},{5,6},{6,7},{7,8},{8,9},{9,10},{10,1... | collective-permute-start | bytes 1572872 | tf_op jit(solution)/shard_map/ppermute | solution.py:20
  15.9 16.2 %collective-permute-start.1 = (bf16[512,512]{1,0:T(8,128)(2,1)S(1)}, bf16[512,512]{1,0:T(8,128)(2,1)S(1)}, u32[]{:S(2)}, u32[]{:S(2)}) collective-permute-start(bf16[512,512]{1,0:T(8,128)(2,1)S(1)} %get-tuple-element.93), channel_id=1, source_target_pairs={{0,15},{1,0},{2,1},{3,2},{4,3},{5,4},{6,5},{7,6},{8,7},{9,8},{10,9... | collective-permute-start | bytes 1572872 | tf_op jit(solution)/shard_map/ppermute | solution.py:23
  32.1 15.5 %collective-permute-start.2 = (bf16[512,512]{1,0:T(8,128)(2,1)S(1)}, bf16[512,512]{1,0:T(8,128)(2,1)S(1)}, u32[]{:S(2)}, u32[]{:S(2)}) collective-permute-start(bf16[512,512]{1,0:T(8,128)(2,1)S(1)} %collective-permute-done), channel_id=1, source_target_pairs={{0,1},{1,2},{2,3},{3,4},{4,5},{5,6},{6,7},{7,8},{8,9},{9,10},{10,1... | collective-permute-start | bytes 1572872 | tf_op jit(solution)/shard_map/ppermute | solution.py:20
  32.1 15.5 %copy-start.3 = (bf16[512,512]{1,0:T(8,128)(2,1)}, bf16[512,512]{1,0:T(8,128)(2,1)S(1)}, u32[]{:S(2)}) copy-start(bf16[512,512]{1,0:T(8,128)(2,1)S(1)} %collective-permute-done.1) | copy-start | bytes 1572868
  32.1 15.5 %collective-permute-start.3 = (bf16[512,512]{1,0:T(8,128)(2,1)S(1)}, bf16[512,512]{1,0:T(8,128)(2,1)S(1)}, u32[]{:S(2)}, u32[]{:S(2)}) collective-permute-start(bf16[512,512]{1,0:T(8,128)(2,1)S(1)} %collective-permute-done.1), channel_id=1, source_target_pairs={{0,15},{1,0},{2,1},{3,2},{4,3},{5,4},{6,5},{7,6},{8,7},{9,8},{10,9... | collective-permute-start | bytes 1572872 | tf_op jit(solution)/shard_map/ppermute | solution.py:23
  47.6 4.9 copy-start.5
  47.6 14.6 %collective-permute-start.4 = (bf16[512,512]{1,0:T(8,128)(2,1)S(1)}, bf16[512,512]{1,0:T(8,128)(2,1)S(1)}, u32[]{:S(2)}, u32[]{:S(2)}) collective-permute-start(bf16[512,512]{1,0:T(8,128)(2,1)S(1)} %collective-permute-done.2), channel_id=1, source_target_pairs={{0,1},{1,2},{2,3},{3,4},{4,5},{5,6},{6,7},{7,8},{8,9},{9,10},{10,1... | collective-permute-start | bytes 1572872 | tf_op jit(solution)/shard_map/ppermute | solution.py:20
  47.6 28.2 %copy-start.2 = (bf16[512,512]{1,0:T(8,128)(2,1)}, bf16[512,512]{1,0:T(8,128)(2,1)S(1)}, u32[]{:S(2)}) copy-start(bf16[512,512]{1,0:T(8,128)(2,1)S(1)} %collective-permute-done.3) | copy-start | bytes 1572868
  47.6 14.6 %collective-permute-start.5 = (bf16[512,512]{1,0:T(8,128)(2,1)S(1)}, bf16[512,512]{1,0:T(8,128)(2,1)S(1)}, u32[]{:S(2)}, u32[]{:S(2)}) collective-permute-start(bf16[512,512]{1,0:T(8,128)(2,1)S(1)} %collective-permute-done.3), channel_id=1, source_target_pairs={{0,15},{1,0},{2,1},{3,2},{4,3},{5,4},{6,5},{7,6},{8,7},{9,8},{10,9... | collective-permute-start | bytes 1572872 | tf_op jit(solution)/shard_map/ppermute | solution.py:23
  62.2 13.7 %collective-permute-start.6 = (bf16[512,512]{1,0:T(8,128)(2,1)S(1)}, bf16[512,512]{1,0:T(8,128)(2,1)S(1)}, u32[]{:S(2)}, u32[]{:S(2)}) collective-permute-start(bf16[512,512]{1,0:T(8,128)(2,1)S(1)} %collective-permute-done.4), channel_id=1, source_target_pairs={{0,1},{1,2},{2,3},{3,4},{4,5},{5,6},{6,7},{7,8},{8,9},{9,10},{10,1... | collective-permute-start | bytes 1572872 | tf_op jit(solution)/shard_map/ppermute | solution.py:20
  62.2 13.7 %collective-permute-start.7 = (bf16[512,512]{1,0:T(8,128)(2,1)S(1)}, bf16[512,512]{1,0:T(8,128)(2,1)}, u32[]{:S(2)}, u32[]{:S(2)}) collective-permute-start(bf16[512,512]{1,0:T(8,128)(2,1)S(1)} %collective-permute-done.5), channel_id=1, source_target_pairs={{0,15},{1,0},{2,1},{3,2},{4,3},{5,4},{6,5},{7,6},{8,7},{9,8},{10,9... | collective-permute-start | bytes 1572872 | tf_op jit(solution)/shard_map/ppermute | solution.py:23
  75.8 0.8 copy-start.4
  75.8 12.8 %collective-permute-start.8 = (bf16[512,512]{1,0:T(8,128)(2,1)S(1)}, bf16[512,512]{1,0:T(8,128)(2,1)}, u32[]{:S(2)}, u32[]{:S(2)}) collective-permute-start(bf16[512,512]{1,0:T(8,128)(2,1)S(1)} %collective-permute-done.6), channel_id=1, source_target_pairs={{0,1},{1,2},{2,3},{3,4},{4,5},{5,6},{6,7},{7,8},{8,9},{9,10},{10,1... | collective-permute-start | bytes 1572872 | tf_op jit(solution)/shard_map/ppermute | solution.py:20
  76.7 16.8 %collective-permute-start.9 = (bf16[512,512]{1,0:T(8,128)(2,1)}, bf16[512,512]{1,0:T(8,128)(2,1)S(1)}, u32[]{:S(2)}, u32[]{:S(2)}) collective-permute-start(bf16[512,512]{1,0:T(8,128)(2,1)} %collective-permute-done.7), channel_id=1, source_target_pairs={{0,15},{1,0},{2,1},{3,2},{4,3},{5,4},{6,5},{7,6},{8,7},{9,8},{10,9... | collective-permute-start | bytes 1572872 | tf_op jit(solution)/shard_map/ppermute | solution.py:23
  88.7 12.1 %collective-permute-start.10 = (bf16[512,512]{1,0:T(8,128)(2,1)}, bf16[512,512]{1,0:T(8,128)(2,1)}, u32[]{:S(2)}, u32[]{:S(2)}) collective-permute-start(bf16[512,512]{1,0:T(8,128)(2,1)} %collective-permute-done.8), channel_id=1, source_target_pairs={{0,1},{1,2},{2,3},{3,4},{4,5},{5,6},{6,7},{7,8},{8,9},{9,10},{10,1... | collective-permute-start | bytes 1572872 | tf_op jit(solution)/shard_map/ppermute | solution.py:20
  93.5 12.9 %collective-permute-start.11 = (bf16[512,512]{1,0:T(8,128)(2,1)S(1)}, bf16[512,512]{1,0:T(8,128)(2,1)S(1)}, u32[]{:S(2)}, u32[]{:S(2)}) collective-permute-start(bf16[512,512]{1,0:T(8,128)(2,1)S(1)} %collective-permute-done.9), channel_id=1, source_target_pairs={{0,15},{1,0},{2,1},{3,2},{4,3},{5,4},{6,5},{7,6},{8,7},{9,8},{10,9... | collective-permute-start | bytes 1572872 | tf_op jit(solution)/shard_map/ppermute | solution.py:23
  100.8 12.4 %collective-permute-start.12 = (bf16[512,512]{1,0:T(8,128)(2,1)}, bf16[512,512]{1,0:T(8,128)(2,1)S(1)}, u32[]{:S(2)}, u32[]{:S(2)}) collective-permute-start(bf16[512,512]{1,0:T(8,128)(2,1)} %collective-permute-done.10), channel_id=1, source_target_pairs={{0,1},{1,2},{2,3},{3,4},{4,5},{5,6},{6,7},{7,8},{8,9},{9,10},{10,1... | collective-permute-start | bytes 1572872 | tf_op jit(solution)/shard_map/ppermute | solution.py:20
  106.4 11.4 %collective-permute-start.13 = (bf16[512,512]{1,0:T(8,128)(2,1)S(1)}, bf16[512,512]{1,0:T(8,128)(2,1)S(1)}, u32[]{:S(2)}, u32[]{:S(2)}) collective-permute-start(bf16[512,512]{1,0:T(8,128)(2,1)S(1)} %collective-permute-done.11), channel_id=1, source_target_pairs={{0,15},{1,0},{2,1},{3,2},{4,3},{5,4},{6,5},{7,6},{8,7},{9,8},{10,9... | collective-permute-start | bytes 1572872 | tf_op jit(solution)/shard_map/ppermute | solution.py:23
  113.2 11.4 %collective-permute-start.14 = (bf16[512,512]{1,0:T(8,128)(2,1)S(1)}, bf16[512,512]{1,0:T(8,128)(2,1)S(1)}, u32[]{:S(2)}, u32[]{:S(2)}) collective-permute-start(bf16[512,512]{1,0:T(8,128)(2,1)S(1)} %collective-permute-done.12), channel_id=1, source_target_pairs={{0,1},{1,2},{2,3},{3,4},{4,5},{5,6},{6,7},{7,8},{8,9},{9,10},{10,1... | collective-permute-start | bytes 1572872 | tf_op jit(solution)/shard_map/ppermute | solution.py:20
  348.3 0.7 copy-start.7
  348.3 225.8 %all-gather.2.cloned.1.call-start = ((), (), s32[]{:S(2)}) async-start(), calls=%async_computation.1 | async-start | bytes 4718592 | tf_op jit(solution)/shard_map/all_gather | solution.py:58
Sparse Core Ops, SparseCore 0:
  348.4 223.4 all-reduce.1
Sparse Core Ops, SparseCore 1:
  350.5 35.4 all-gather.1
